TPU v7x, 32 devices: a whole 2x2x4 slice. The times are simulated.
32 devices in a mesh: row: 8 (over z, y), col: 4 (over x, core).
Axes of the slice: x: 2, y: 2, z: 4, core: 2. Of those that a mesh axis runs over, the one named last changes fastest.
Arguments:
- tensor: bfloat16 [2048, 8192], P(('row', 'col')), may hold values from -6 to 6
- density: bfloat16 [2, 4096, 8192], P(None, 'col', 'row'), may hold values from -0.125 to 0.125
- tensor_mask: int32 [16, 64], replicated, may hold values 0 or 1
- density_mask: int32 [64, 64], replicated, may hold values 0 or 1
- pair_rows: int32 [32], replicated, may hold values from 0 to 31, as said below
Outputs:
- contracted: bfloat16 [2048, 8192], P(('row', 'col'))
Inputs may be any that keep to these rules, and one draw needn't show every extreme that they name: pair_rows is a permutation of 0 to 31. Among the 8 slots that share one remainder modulo 4, at most 3 hold units of any one group of 8 consecutive units, and for every remainder some group gets exactly 3.
All inputs are finite; a program needn't handle non-finite values.
Results may differ from a plain program's by a relative error of at most 0.001.
Values may be sent and summed in bfloat16 or wider, within the bound.
A program may use at most 64 MiB of HBM per device.

v0:
```python
import jax
import jax.numpy as jnp
from jax import lax
from jax.sharding import PartitionSpec as P

BLOCK = 128


def on_device(tensor, density, tensor_mask, density_mask, pair_rows):
    row_count = lax.axis_size("row")
    col_count = lax.axis_size("col")
    row_index = lax.axis_index("row")
    col_index = lax.axis_index("col")
    unit_rows, orbitals = tensor.shape
    owner_slot = row_index * col_count + col_index
    own_unit = pair_rows[owner_slot]
    mask_rows = (own_unit * unit_rows + jnp.arange(unit_rows, dtype=jnp.int32)) // BLOCK
    row_mask = jnp.repeat(
        jnp.take(tensor_mask, mask_rows, axis=0).astype(jnp.bfloat16), BLOCK, axis=1
    )
    masked = tensor * row_mask
    piece_rows = density.shape[1]
    piece_width = density.shape[2]
    half_rows = orbitals // 2
    global_rows = (
        jnp.arange(2)[:, None] * half_rows
        + col_index * piece_rows
        + jnp.arange(piece_rows)[None, :]
    )
    global_cols = row_index * piece_width + jnp.arange(piece_width)
    dens_mask = jnp.take(
        jnp.take(density_mask, (global_rows // BLOCK).reshape(-1), axis=0),
        global_cols // BLOCK,
        axis=1,
    )
    density_pair = density * dens_mask.reshape(2, piece_rows, piece_width).astype(jnp.bfloat16)
    column = lax.all_gather(density_pair, "col", axis=1, tiled=True).reshape(orbitals, piece_width)
    tile_result = jnp.dot(
        lax.all_gather(masked, "row", axis=0, tiled=True),
        column,
        preferred_element_type=jnp.float32,
    ).astype(jnp.bfloat16)
    tile_result = tile_result.reshape(row_count, unit_rows, piece_width)
    owned_rows = lax.all_to_all(tile_result, "row", split_axis=0, concat_axis=2, tiled=True)
    return owned_rows.reshape(unit_rows, orbitals)


def solution(mesh):
    placed = (P(("row", "col"), None), P(None, "col", "row"), P(), P(), P())
    return jax.shard_map(
        on_device, mesh=mesh, in_specs=placed, out_specs=P(("row", "col"), None), check_vma=False
    )
```

profile of v0, /device:TPU:0, one launch (start us, length us, event | category | flops | bytes accessed | tf_op | source)
XLA Modules:
  0.0 300.5 jit_solution(1032798503816356706)
XLA Ops:
  6.5 0.0 copy-start
  6.5 0.0 all-gather.3.cloned.1.call-start
  6.5 1.2 dynamic_slice.3
  8.5 1.3 gather_fusion
  9.8 0.1 select_convert_fusion.1
  9.9 0.6 broadcast_in_dim.37
  10.5 2.9 bitcast_multiply_fusion
  13.4 0.0 all-gather.3.cloned.1.call-update
  13.4 0.0 all-gather.5.cloned.1.call-start
  13.5 0.1 fusion.4
  13.6 0.0 copy-done
  13.6 5.5 %gather_fusion.1 = s32[2048,64]{1,0:T(8,128)S(1)} fusion(s32[64,64]{1,0:T(8,128)S(1)} %copy-done, s32[2048]{0:T(1024)S(1)} %broadcast_clamp_fusion), kind=kCustom, calls=%fused_computation.1 | custom fusion | bytes 1056768 | tf_op jit(solution)/shard_map/jit(_take)/gather | solution.py:32
  19.1 0.3 broadcast_select_fusion
  19.5 0.3 copy.9
  19.8 6.8 %gather_fusion.2 = s32[1024,2048]{1,0:T(8,128)} fusion(s32[2048,64]{0,1:T(8,128)S(1)} %copy.9, s32[1024]{0:T(1024)S(1)} %broadcast_clamp_fusion.1), kind=kCustom, calls=%fused_computation.2 | custom fusion | bytes 16781312 | tf_op jit(solution)/shard_map/jit(_take)/gather | solution.py:31
  26.7 9.3 %copy.12 = s32[2048,1024]{1,0:T(8,128)} copy(s32[2048,1024]{0,1:T(8,128)} %bitcast.47) | data formatting | bytes 16777216 | tf_op jit(solution)/shard_map/jit(_take)/gather | solution.py:31
  36.0 8.3 %fusion = bf16[2,1024,1024]{2,1,0:T(8,128)(2,1)} fusion(bf16[2,1024,1024]{2,1,0:T(8,128)(2,1)} %param.6, s32[2,1024,1024]{2,1,0:T(8,128)} %bitcast.48, pred[1024]{0:T(1024)(128)(4,1)S(1)} %compare_and_fusion.1), kind=kLoop, calls=%fused_computation.4 | loop fusion | flops 6291456 | bytes 16778240 | tf_op jit(solution)/shard_map/mul | solution.py:36
  44.3 0.0 all-gather.5.cloned.1.call-update
  44.3 96.4 %all-gather.3.cloned.1.call-done = bf16[512,8192]{1,0:T(8,128)(2,1)} async-done(((bf16[64,8192]{1,0:T(8,128)(2,1)}), bf16[512,8192]{1,0:T(8,128)(2,1)}) %all-gather.3.cloned.1.call-update) | async-done | bytes 8388624 | tf_op jit(solution)/shard_map/all_gather | solution.py:39
  140.7 105.7 %all-gather.5.cloned.1.call-done = bf16[2,4096,1024]{2,1,0:T(8,128)(2,1)} async-done(((bf16[2,1024,1024]{2,1,0:T(8,128)(2,1)}), bf16[2,4096,1024]{2,1,0:T(8,128)(2,1)}) %all-gather.5.cloned.1.call-update) | async-done | bytes 16777232 | tf_op jit(solution)/shard_map/all_gather | solution.py:37
  246.4 14.8 %convolution_convert_fusion = bf16[512,1024]{1,0:T(8,128)(2,1)S(1)} fusion(bf16[512,8192]{1,0:T(8,128)(2,1)} %all-gather.3.cloned.1.call-done, bf16[8192,1024]{1,0:T(8,128)(2,1)} %bitcast.55), kind=kOutput, calls=%fused_computation.5 | convolution fusion | flops 8590458880 | bytes 26214400 | tf_op jit(solution)/shard_map/dot_general | solution.py:38
  261.2 31.4 %all_to_all.15 = bf16[8,64,1024]{2,1,0:T(8,128)(2,1)S(1)} all-to-all(bf16[8,64,1024]{2,1,0:T(8,128)(2,1)S(1)} %bitcast.51), channel_id=1, replica_groups=mesh['row'=8,'col'=4] {'row'}, dimensions={0} | all-to-all | bytes 2097152 | tf_op jit(solution)/shard_map/all_to_all | solution.py:44
  292.6 1.1 copy.16
  (11 shorter events, 0.2 us)
Async XLA Ops:
  6.5 7.1 %copy-start = (s32[64,64]{1,0:T(8,128)S(1)}, s32[64,64]{1,0:T(8,128)}, u32[]{:S(2)}) copy-start(s32[64,64]{1,0:T(8,128)} %param.8) | copy-start | bytes 49156
  6.5 134.2 %all-gather.3.cloned.1.call-start = ((), (), s32[]{:S(2)}) async-start(), calls=%async_computation.1 | async-start | bytes 9437184 | tf_op jit(solution)/shard_map/all_gather | solution.py:39
  13.4 233.0 %all-gather.5.cloned.1.call-start = ((), (), s32[]{:S(2)}) async-start(), calls=%async_computation.2 | async-start | bytes 20971520 | tf_op jit(solution)/shard_map/all_gather | solution.py:37
Sparse Core Ops, SparseCore 0:
  13.5 127.1 all-gather.2
  142.3 104.0 all-gather.4
where the time goes:
time: 301 us
  waiting for transfers between devices  202 us (67%)
  blocking collectives  31.4 us (10%)
  local copies, waits for them, and re-layouts  26.1 us (9%)
  matrix products  14.8 us (5%)
  between operations  14.2 us (5%)
  other arithmetic  11.8 us (4%)
    all_gather x1, waiting for transfers between devices, on_device(): lax.all_gather(density_pair, 'col', axis=1, tiled=True)  106 us
    all_gather x1, waiting for transfers between devices, on_device(): lax.all_gather(masked, 'row', axis=0, tiled=True)  96.4 us
    all_to_all x1, blocking collectives, on_device(): lax.all_to_all(tile_result, 'row', split_axis=0, concat_axis=2, tiled=True)  31.4 us
    gather x2, local copies, waits for them, and re-layouts, on_device(): jnp.take(jnp.take(density_mask, (global_rows // BLOCK).reshape(-1), axis=...  16.1 us
    dot_general x1, matrix products, on_device(): jnp.dot(lax.all_gather(masked, 'row', axis=0, tiled=True), column, prefer...  14.8 us
    mul x1, other arithmetic, on_device(): density * dens_mask.reshape(2, piece_rows, piece_width).astype(jnp.bfloat16)  8.29 us
  transfers between devices with their start and end apart: 2, of which 2 were waited for; matrix products, arithmetic and copies ran while one was open for 10% of the time, Pallas kernels for 0%

commit v1 on v0

--- a/solution.py
+++ b/solution.py
@@ -34,7 +34,9 @@
         axis=1,
     )
     density_pair = density * dens_mask.reshape(2, piece_rows, piece_width).astype(jnp.bfloat16)
-    column = lax.all_gather(density_pair, "col", axis=1, tiled=True).reshape(orbitals, piece_width)
+    column = jnp.concatenate(lax.all_gather(density_pair, "col"), axis=1).reshape(
+        orbitals, piece_width
+    )
     tile_result = jnp.dot(
         lax.all_gather(masked, "row", axis=0, tiled=True),
         column,

time: 301 us -> 325 us (1.080)
  waiting for transfers between devices: 202 us -> 217 us
  local copies, waits for them, and re-layouts: 26.1 us -> 39.3 us
    all_gather x1, waiting for transfers between devices: 96.4 us -> 113 us  [on_device(): lax.all_gather(masked, 'row', axis=0, tiled=True)]
    reshape x0 -> x1, local copies, waits for them, and re-layouts: none -> 14 us  [on_device(): jnp.concatenate(lax.all_gather(density_pair, 'col'), axis=1)]
  transfers between devices with their start and end apart: 2 -> 2, of which waited for: 2 -> 2; matrix products, arithmetic and copies ran while one was open for 10% -> 5% of each run, Pallas kernels for 0% -> 0%
where the time goes in v1:
time: 325 us; the launch traced here: 324 us
  waiting for transfers between devices  217 us (67%)
  local copies, waits for them, and re-layouts  39.3 us (12%)
  blocking collectives  28.3 us (9%)
  matrix products  14.8 us (5%)
  between operations  14.2 us (4%)
  other arithmetic  10.6 us (3%)
    all_gather x1, waiting for transfers between devices, on_device(): lax.all_gather(masked, 'row', axis=0, tiled=True)  113 us
    all_gather x1, waiting for transfers between devices, on_device(): lax.all_gather(density_pair, 'col')  104 us
    all_to_all x1, blocking collectives, on_device(): lax.all_to_all(tile_result, 'row', split_axis=0, concat_axis=2, tiled=True)  28.3 us
    gather x2, local copies, waits for them, and re-layouts, on_device(): jnp.take(jnp.take(density_mask, (global_rows // BLOCK).reshape(-1), axis=...  16.1 us
    dot_general x1, matrix products, on_device(): jnp.dot(lax.all_gather(masked, 'row', axis=0, tiled=True), column, prefer...  14.8 us
    reshape x1, local copies, waits for them, and re-layouts, on_device(): jnp.concatenate(lax.all_gather(density_pair, 'col'), axis=1)  14 us
    mul x1, other arithmetic, on_device(): density * dens_mask.reshape(2, piece_rows, piece_width).astype(jnp.bfloat16)  8.28 us
  transfers between devices with their start and end apart: 2, of which 2 were waited for; matrix products, arithmetic and copies ran while one was open for 5% of the time, Pallas kernels for 0%

profile of v1, /device:TPU:0, one launch (start us, length us, event | category | flops | bytes accessed | tf_op | source)
XLA Modules:
  0.0 324.3 jit_solution(9262958949079658965)
XLA Ops:
  6.6 0.1 fusion.4
  6.8 0.5 copy-done
  7.3 5.5 %gather_fusion.1 = s32[2048,64]{1,0:T(8,128)S(1)} fusion(s32[64,64]{1,0:T(8,128)S(1)} %copy-done, s32[2048]{0:T(1024)S(1)} %broadcast_clamp_fusion), kind=kCustom, calls=%fused_computation.1 | custom fusion | bytes 1056768 | tf_op jit(solution)/shard_map/jit(_take)/gather | solution.py:32
  12.8 0.3 broadcast_select_fusion
  13.1 0.3 copy.16
  13.4 6.9 %gather_fusion.2 = s32[1024,2048]{1,0:T(8,128)} fusion(s32[2048,64]{0,1:T(8,128)S(1)} %copy.16, s32[1024]{0:T(1024)S(1)} %broadcast_clamp_fusion.1), kind=kCustom, calls=%fused_computation.2 | custom fusion | bytes 16781312 | tf_op jit(solution)/shard_map/jit(_take)/gather | solution.py:31
  20.3 9.3 %copy.20 = s32[2048,1024]{1,0:T(8,128)} copy(s32[2048,1024]{0,1:T(8,128)} %bitcast.50) | data formatting | bytes 16777216 | tf_op jit(solution)/shard_map/jit(_take)/gather | solution.py:31
  29.6 8.3 %fusion = bf16[2,1024,1024]{2,1,0:T(8,128)(2,1)} fusion(bf16[2,1024,1024]{2,1,0:T(8,128)(2,1)} %param.6, s32[2,1024,1024]{2,1,0:T(8,128)} %bitcast.51, pred[1024]{0:T(1024)(128)(4,1)S(1)} %compare_and_fusion.1), kind=kLoop, calls=%fused_computation.4 | loop fusion | flops 6291456 | bytes 16778240 | tf_op jit(solution)/shard_map/mul | solution.py:36
  37.8 0.0 all-gather.6.cloned.1.call-update
  37.9 0.0 all-gather.4.cloned.1.call-start
  37.9 0.0 copy-done.4
  37.9 0.6 dynamic_slice.3
  39.2 0.0 copy-done.2
  39.2 0.6 gather_fusion
  39.8 0.1 select_convert_fusion.1
  39.9 0.6 broadcast_in_dim.37
  40.5 1.7 bitcast_multiply_fusion
  42.2 0.0 all-gather.4.cloned.1.call-update
  42.2 104.4 %all-gather.6.cloned.1.call-done = bf16[8,1024,1024]{2,1,0:T(8,128)(2,1)} async-done(((bf16[2,1024,1024]{2,1,0:T(8,128)(2,1)}), bf16[8,1024,1024]{2,1,0:T(8,128)(2,1)}) %all-gather.6.cloned.1.call-update) | async-done | bytes 16777232 | tf_op jit(solution)/shard_map/all_gather | solution.py:37
  146.6 14.0 %copy.18 = bf16[2,4,1024,1024]{3,2,1,0:T(8,128)(2,1)} copy(bf16[2,4,1024,1024]{3,2,0,1:T(8,128)(2,1)} %bitcast.52) | data formatting | bytes 33554432 | tf_op jit(solution)/shard_map/reshape | solution.py:37
  160.7 112.6 %all-gather.4.cloned.1.call-done = bf16[512,8192]{1,0:T(8,128)(2,1)} async-done(((bf16[64,8192]{1,0:T(8,128)(2,1)}), bf16[512,8192]{1,0:T(8,128)(2,1)}) %all-gather.4.cloned.1.call-update) | async-done | bytes 8388624 | tf_op jit(solution)/shard_map/all_gather | solution.py:41
  273.3 14.8 %convolution_convert_fusion = bf16[512,1024]{1,0:T(8,128)(2,1)S(1)} fusion(bf16[512,8192]{1,0:T(8,128)(2,1)} %all-gather.4.cloned.1.call-done, bf16[8192,1024]{1,0:T(8,128)(2,1)} %bitcast.53), kind=kOutput, calls=%fused_computation.5 | convolution fusion | flops 8590458880 | bytes 26214400 | tf_op jit(solution)/shard_map/dot_general | solution.py:40
  288.1 28.3 %all_to_all.15 = bf16[8,64,1024]{2,1,0:T(8,128)(2,1)S(1)} all-to-all(bf16[8,64,1024]{2,1,0:T(8,128)(2,1)S(1)} %bitcast.56), channel_id=1, replica_groups=mesh['row'=8,'col'=4] {'row'}, dimensions={0} | all-to-all | bytes 2097152 | tf_op jit(solution)/shard_map/all_to_all | solution.py:46
  316.4 1.1 copy.24
  (19 shorter events, 0.2 us)
Async XLA Ops:
  6.5 0.8 copy-start
  6.5 140.1 %all-gather.6.cloned.1.call-start = ((), (), s32[]{:S(2)}) async-start(), calls=%async_computation.2 | async-start | bytes 20971520 | tf_op jit(solution)/shard_map/all_gather | solution.py:37
  29.6 8.4 %copy-start.4 = (s32[32]{0:T(128)S(1)}, s32[32]{0:T(128)}, u32[]{:S(2)}) copy-start(s32[32]{0:T(128)} %param.9) | copy-start | bytes 388
  29.6 9.6 %copy-start.2 = (s32[16,64]{1,0:T(8,128)S(1)}, s32[16,64]{1,0:T(8,128)}, u32[]{:S(2)}) copy-start(s32[16,64]{1,0:T(8,128)} %param.7) | copy-start | bytes 12292
  29.6 11.0 %copy-start.3 = (bf16[64,8192]{1,0:T(8,128)(2,1)S(1)}, bf16[64,8192]{1,0:T(8,128)(2,1)}, u32[]{:S(2)}) copy-start(bf16[64,8192]{1,0:T(8,128)(2,1)} %param.5) | copy-start | bytes 3145732
  37.9 235.4 %all-gather.4.cloned.1.call-start = ((), (), s32[]{:S(2)}) async-start(), calls=%async_computation.1 | async-start | bytes 9437184 | tf_op jit(solution)/shard_map/all_gather | solution.py:41
  273.3 44.2 %copy-start.1 = (s32[64,64]{1,0:T(8,128)S(1)}, s32[64,64]{1,0:T(8,128)}, u32[]{:S(2)}) copy-start(s32[64,64]{1,0:T(8,128)} %param.8) | copy-start | bytes 49156
Sparse Core Ops, SparseCore 0:
  38.0 108.6 all-gather.5
  148.8 124.4 all-gather.3
